TPU v7x, 32 devices: a whole 2x2x4 slice. The times are simulated.
32 devices in a mesh: grp: 2 (over x), refl: 16 (over z, y, core).
Axes of the slice: x: 2, y: 2, z: 4, core: 2. Of those that a mesh axis runs over, the one named last changes fastest.
Arguments:
- feed_plane: float32 [4, 2048], P('grp', 'refl'), parts along dimension 0, may hold values from -3 to 3
- feed_height: float32 [4096], P(('grp', 'refl')), parts along dimension 0, may hold values from 20 to 24
- feed_weights: bfloat16 [2048, 256], P('refl', 'grp'), parts along dimension 1, may hold values from -0.125 to 0.125
- point_plane: float32 [4, 4096], P('grp', 'refl'), parts along dimension 0, may hold values from -35 to 35
- point_height: float32 [8192], P(('grp', 'refl')), parts along dimension 0, may hold values from 0 to 4
- patch_factor: float32 [8192], P(('grp', 'refl')), parts along dimension 0, may hold values from 0.3 to 3
- direction_cosines: float32 [2, 2048], P(None, 'refl'), may hold values from -0.3 to 0.3
Outputs:
- pattern: float32 [2048, 256], P('refl', 'grp'), parts along dimension 1
There are 2 independent parts, one for each index of `grp`. A program takes and returns all parts, laid end to end along the dimension named above; an argument that names none is the same for every part. Nothing has to cross between parts.
All inputs are finite; a program needn't handle non-finite values.
Results may differ from a plain program's by a relative error of at most 0.0047.
Values may be sent and summed in bfloat16 or wider, within the bound.
A program may use at most 64 MiB of HBM per device.

v0:
```python
import math

import jax
import jax.numpy as jnp
from jax import lax
from jax.sharding import PartitionSpec as P

TWO_PI = 2.0 * math.pi
RANGE_REF = 20.0


def rotate(columns):
    half = columns.shape[1] // 2
    return jnp.concatenate([-columns[:, half:], columns[:, :half]], axis=1)


def green_tile(point_plane, point_height, feed_plane, feed_height):
    across = point_plane[0][:, None] - feed_plane[0][None, :]
    along = point_plane[1][:, None] - feed_plane[1][None, :]
    height = feed_height[None, :] - point_height[:, None]
    squared = across * across + along * along + height * height
    distance = jnp.sqrt(squared)
    amplitude = RANGE_REF * height / squared
    turning = TWO_PI * distance
    return (
        (amplitude * jnp.cos(turning)).astype(jnp.bfloat16),
        (-amplitude * jnp.sin(turning)).astype(jnp.bfloat16),
    )


def incident_rows(point_plane, point_height, feed_plane, feed_height, weights, weights_turned):
    in_phase, quadrature = green_tile(point_plane, point_height, feed_plane, feed_height)
    return jnp.dot(in_phase, weights, preferred_element_type=jnp.float32) + jnp.dot(
        quadrature, weights_turned, preferred_element_type=jnp.float32
    )


def far_kernel(cosines, point_plane, point_height):
    normal = jnp.sqrt(1.0 - cosines[0] * cosines[0] - cosines[1] * cosines[1])
    turning = TWO_PI * (
        cosines[0][:, None] * point_plane[0][None, :]
        + cosines[1][:, None] * point_plane[1][None, :]
        + normal[:, None] * point_height[None, :]
    )
    return (jnp.cos(turning).astype(jnp.bfloat16), jnp.sin(turning).astype(jnp.bfloat16))


def radiate_rows(cosines, point_plane, point_height, currents, currents_turned):
    in_phase, quadrature = far_kernel(cosines, point_plane, point_height)
    return jnp.dot(in_phase, currents, preferred_element_type=jnp.float32) + jnp.dot(
        quadrature, currents_turned, preferred_element_type=jnp.float32
    )


def per_device(
    feed_plane,
    feed_height,
    feed_weights,
    point_plane,
    point_height,
    patch_factor,
    direction_cosines,
):
    local_points = point_plane.shape[1]
    source_plane, source_height = (
        lax.all_gather(feed_plane, "refl", axis=1, tiled=True),
        lax.all_gather(feed_height, "refl", axis=0, tiled=True),
    )
    segment = lax.all_gather(feed_weights, "refl", axis=0, tiled=True)
    part_plane = source_plane
    part_height = source_height
    incident = incident_rows(
        point_plane, point_height, part_plane, part_height, segment, rotate(segment)
    )
    norm_scale = 1.0 / math.sqrt(local_points * lax.axis_size("refl"))
    currents = (incident * (patch_factor * norm_scale)[:, None]).astype(jnp.bfloat16)
    radiator_plane, radiator_height = (
        lax.all_gather(point_plane, "refl", axis=1, tiled=True),
        lax.all_gather(point_height, "refl", axis=0, tiled=True),
    )
    segment = lax.all_gather(currents, "refl", axis=0, tiled=True)
    part_plane = radiator_plane
    part_height = radiator_height
    return radiate_rows(direction_cosines, part_plane, part_height, segment, rotate(segment))


def solution(mesh):
    in_specs = (
        P("grp", "refl"),
        P(("grp", "refl")),
        P("refl", "grp"),
        P("grp", "refl"),
        P(("grp", "refl")),
        P(("grp", "refl")),
        P(None, "refl"),
    )
    out_specs = P("refl", "grp")
    return jax.shard_map(
        per_device, mesh=mesh, in_specs=in_specs, out_specs=out_specs, check_vma=False
    )
```

profile of v0, /device:TPU:0, one launch (start us, length us, event | category | flops | bytes accessed | tf_op | source)
XLA Modules:
  0.0 149.6 jit_solution(372851326946409768)
XLA Ops:
  6.5 0.0 all-gather.4.cloned.1.call-start
  6.5 0.7 broadcast_multiply_fusion
  7.2 0.8 fusion.36
  8.0 23.3 %all-gather.1 = f32[16,1,128]{2,1,0:T(1,128)S(1)} all-gather(f32[1,1,128]{2,1,0:T(1,128)} %bitcast.37), channel_id=1, replica_groups=mesh['grp'=2,'refl'=16] {'refl'}, dimensions={0}, use_global_device_ids=true | all-gather | bytes 8704 | tf_op jit(solution)/shard_map/all_gather | solution.py:67
  31.3 17.7 %all_gather.21 = f32[2,2048]{1,0:T(2,128)S(1)} all-gather(f32[2,128]{1,0:T(2,128)} %param.7), channel_id=1, replica_groups=mesh['grp'=2,'refl'=16] {'refl'}, dimensions={1}, use_global_device_ids=true | all-gather | bytes 17408 | tf_op jit(solution)/shard_map/all_gather | solution.py:66
  49.0 20.5 %all_gather.22 = bf16[2048,128]{1,0:T(8,128)(2,1)S(1)} all-gather(bf16[128,128]{1,0:T(8,128)(2,1)} %param.9), channel_id=1, replica_groups=mesh['grp'=2,'refl'=16] {'refl'}, dimensions={0}, use_global_device_ids=true | all-gather | bytes 557056 | tf_op jit(solution)/shard_map/all_gather | solution.py:69
  69.5 0.0 copy-start.2
  69.5 0.2 slice_negate_fusion.1
  69.7 0.4 copy-done.2
  70.2 8.3 %fusion.22 = f32[256,128]{1,0:T(8,128)S(1)} fusion(bf16[2048,128]{1,0:T(8,128)(2,1)S(1)} %all_gather.22, f32[2048]{0:T(1024)S(1)} %bitcast.30, f32[256]{0:T(256)S(1)} %bitcast.35, f32[2048]{0:T(1024)S(1)} %bitcast.28, f32[256]{0:T(256)S(1)} %bitcast.33, f32[256]{0:T(256)S(1)} %copy-done.2, f32[2048]{0:T(1024)S(1)} %bitcast.26), kind=kOutput, calls=%fused_computation.33 | convolution fusion | flops 141033472 | bytes 683008 | tf_op jit(solution)/shard_map/dot_general | solution.py:33
  78.5 0.0 copy-start.1
  78.5 0.0 copy-start.3
  78.5 9.6 %fusion.3 = bf16[256,128]{1,0:T(8,128)(2,1)} fusion(f32[256,128]{1,0:T(8,128)S(1)} %fusion.22, f32[2048]{0:T(1024)S(1)} %bitcast.31, f32[256]{0:T(256)S(1)} %bitcast.36, f32[2048]{0:T(1024)S(1)} %bitcast.29, f32[256]{0:T(256)S(1)} %bitcast.34, f32[256]{0:T(256)S(1)} %copy-done.2, f32[2048]{0:T(1024)S(1)} %bitcast.27, ...), kind=kOutput, calls=%fused_computation.12 | convolution fusion | flops 142704640 | bytes 749568 | tf_op jit(solution)/shard_map/dot_general | solution.py:33
  88.1 0.0 all-gather.4.cloned.1.call-update
  88.1 17.5 %all-gather = f32[16,1,256]{2,1,0:T(1,128)S(1)} all-gather(f32[1,1,256]{2,1,0:T(1,128)S(1)} %bitcast.32), channel_id=1, replica_groups=mesh['grp'=2,'refl'=16] {'refl'}, dimensions={0}, use_global_device_ids=true | all-gather | bytes 17408 | tf_op jit(solution)/shard_map/all_gather | solution.py:79
  105.6 0.0 copy-done.1
  105.6 18.8 %all_gather.18 = f32[2,4096]{1,0:T(2,128)S(1)} all-gather(f32[2,256]{1,0:T(2,128)S(1)} %copy-done.1), channel_id=1, replica_groups=mesh['grp'=2,'refl'=16] {'refl'}, dimensions={1}, use_global_device_ids=true | all-gather | bytes 34816 | tf_op jit(solution)/shard_map/all_gather | solution.py:78
  124.4 0.0 copy-done.3
  124.4 0.0 all-gather.4.cloned.1.call-done
  124.5 0.0 copy-start
  124.5 2.1 %slice_negate_fusion = (bf16[4096,64]{1,0:T(8,128)(2,1)S(1)}, bf16[4096,64]{1,0:T(8,128)(2,1)S(1)}) fusion(bf16[4096,128]{1,0:T(8,128)(2,1)} %all-gather.4.cloned.1.call-done), kind=kLoop, calls=%fused_computation.15 | loop fusion | flops 262144 | bytes 2097152 | tf_op jit(solution)/shard_map/neg | solution.py:14
  126.5 0.0 copy-done
  126.6 7.4 %fusion.4 = f32[128,128]{1,0:T(8,128)S(1)} fusion(bf16[4096,128]{1,0:T(8,128)(2,1)S(1)} %copy-done, f32[4096]{0:T(1024)S(1)} %bitcast.20, f32[128]{0:T(128)S(1)} %subtract_sqrt_fusion, f32[4096]{0:T(1024)S(1)} %bitcast.24, f32[128]{0:T(128)S(1)} %get-tuple-element.16, f32[4096]{0:T(1024)S(1)} %bitcast.22, f32[128]{0:T(128)S(1)} %get-tuple-element.15), kind=kOutput, calls=%fused_computation.14 | convolution fusion | flops 137887744 | bytes 1164800 | tf_op jit(solution)/shard_map/dot_general | solution.py:50
  133.9 8.9 %convolution_add_fusion.1 = f32[128,128]{1,0:T(8,128)} fusion(f32[128,128]{1,0:T(8,128)S(1)} %fusion.4, bf16[4096,64]{1,0:T(8,128)(2,1)S(1)} %get-tuple-element.6, bf16[4096,64]{1,0:T(8,128)(2,1)S(1)} %get-tuple-element.5, f32[4096]{0:T(1024)S(1)} %bitcast.21, f32[128]{0:T(128)S(1)} %subtract_sqrt_fusion, f32[4096]{0:T(1024)S(1)} %bitcast.25, ...), kind=kOutput, calls=%fused_computation.13 | convolution fusion | flops 140001280 | bytes 1230336 | tf_op jit(solution)/shard_map/dot_general | solution.py:50
  (4 shorter events, 0.1 us)
Async XLA Ops:
  6.5 117.9 %all-gather.4.cloned.1.call-start = ((), (), s32[]{:S(2)}) async-start(), calls=%async_computation | async-start | bytes 1114112 | tf_op jit(solution)/shard_map/all_gather | solution.py:81
  69.5 0.7 copy-start.2
  78.5 27.1 %copy-start.1 = (f32[2,256]{1,0:T(2,128)S(1)}, f32[2,256]{1,0:T(2,128)}, u32[]{:S(2)}) copy-start(f32[2,256]{1,0:T(2,128)} %param.10) | copy-start | bytes 6148
  78.5 45.9 %copy-start.3 = (f32[2,128]{1,0:T(2,128)S(1)}, f32[2,128]{1,0:T(2,128)}, u32[]{:S(2)}) copy-start(f32[2,128]{1,0:T(2,128)} %param.13) | copy-start | bytes 3076
  124.5 2.1 %copy-start = (bf16[4096,128]{1,0:T(8,128)(2,1)S(1)}, bf16[4096,128]{1,0:T(8,128)(2,1)}, u32[]{:S(2)}) copy-start(bf16[4096,128]{1,0:T(8,128)(2,1)} %all-gather.4.cloned.1.call-done) | copy-start | bytes 3145732
Sparse Core Ops, SparseCore 0:
  88.2 35.1 all-gather.3
where the time goes:
time: 150 us
  blocking collectives  97.8 us (65%)
  matrix products  34.1 us (23%)
  between operations  13.4 us (9%)
  other arithmetic  2.98 us (2%)
    all_gather x1, blocking collectives, per_device(): lax.all_gather(feed_height, 'refl', axis=0, tiled=True)  23.3 us
    all_gather x1, blocking collectives, per_device(): segment = lax.all_gather(feed_weights, 'refl', axis=0, tiled=True)  20.5 us
    all_gather x1, blocking collectives, per_device(): lax.all_gather(point_plane, 'refl', axis=1, tiled=True)  18.8 us
    all_gather x1, blocking collectives, per_device(): lax.all_gather(feed_plane, 'refl', axis=1, tiled=True)  17.7 us
    all_gather x1, blocking collectives, per_device(): lax.all_gather(point_height, 'refl', axis=0, tiled=True)  17.5 us
    dot_general x1, matrix products, incident_rows(): jnp.dot(quadrature, weights_turned, preferred_element_type=jnp.float32)  9.56 us
    dot_general x1, matrix products, radiate_rows(): jnp.dot(quadrature, currents_turned, preferred_element_type=jnp.float32)  8.86 us
    dot_general x1, matrix products, incident_rows(): jnp.dot(in_phase, weights, preferred_element_type=jnp.float32)  8.31 us
  transfers between devices with their start and end apart: 1, of which 0 were waited for; matrix products, arithmetic and copies ran while one was open for 0% of the time, Pallas kernels for 0%

commit v1 on v0

v1 whole, which is shorter than its diff:
```python
import functools
import math

import jax
import jax.numpy as jnp
from jax import lax
from jax.experimental import pallas as pl
from jax.experimental.pallas import tpu as pltpu
from jax.sharding import PartitionSpec as P

RANGE_REF = 20.0
GROUP = 4
LANES = 128
ROWS = 32
MESH = pl.DeviceIdType.MESH
ROUNDER = 12582912.0
COS = (0.999999989, -19.7392045, 64.9391159, -85.4501134, 60.1674298, -25.9668846, 6.52770596)
SIN = (6.2831853, -41.3417004, 81.6051308, -76.7030056, 42.0258515, -14.8995784, 3.23778009)


def horner(coefficients, x):
    total = coefficients[-1]
    for c in coefficients[-2::-1]:
        total = total * x + c
    return total


def turn(t):
    r = t - ((t + ROUNDER) - ROUNDER)
    x = r * r
    return horner(COS, x), r * horner(SIN, x)


def rotate(block):
    half = block.shape[1] // 2
    rolled = pltpu.roll(block, half, 1)
    lane = lax.broadcasted_iota(jnp.int32, block.shape, 1)
    return jnp.where(lane < half, -rolled, rolled)


def kernel(
    devices, norm,
    pp_ref, ph_ref, pf_ref, fp_ref, fh_ref, dc_ref, w_ref, out_ref,
    pk, wbuf, gbuf, fbuf, pcol, dcol, fcol, acc, mine, give, take, cbuf, psend, precv,
    pk_send, pk_recv, w_send, w_recv, w_own, x_send, x_recv, c_send, c_recv, p_send, p_recv,
):
    lines, halves = devices // GROUP, devices // 2
    points, sources, dirs = pp_ref.shape[1], fp_ref.shape[1], dc_ref.shape[1]
    me = lax.axis_index("refl")
    line, g = lax.div(me, GROUP), lax.rem(me, GROUP)
    half, core = lax.div(me, 2), lax.rem(me, 2)
    partner = half * 2 + (1 - core)

    def copy(src, dst, send, recv, to):
        return pltpu.make_async_remote_copy(
            src_ref=src, dst_ref=dst, send_sem=send, recv_sem=recv,
            device_id={"refl": to}, device_id_type=MESH,
        )

    halfs = [lax.rem(half + k, halves) for k in range(1, halves)]
    row = lax.rem(half, 2)
    across = (line * 2 + (1 - row)) * 2 + (1 - core)
    peers = [h * 2 + core for h in halfs] + [partner, across]

    barrier = pltpu.get_barrier_semaphore()
    for peer in peers:
        pl.semaphore_signal(barrier, inc=1, device_id={"refl": peer}, device_id_type=MESH)
    own_w = pltpu.make_async_copy(w_ref, wbuf.at[half], w_own)
    own_w.start()

    u, v = dc_ref[0:1, :], dc_ref[1:2, :]
    pk[me, :, :] = jnp.zeros((8, pk.shape[2]), jnp.float32)
    pk[me, 0:2, 0:points] = pp_ref[...]
    pk[me, 2:3, 0:points] = ph_ref[...]
    pk[me, 3:4, 0:points] = pf_ref[...] * norm
    pk[me, 4:6, 0:sources] = fp_ref[...]
    pk[me, 6:7, 0:sources] = fh_ref[...]
    pk[me, 4:6, sources:sources + dirs] = dc_ref[...]
    pk[me, 6:7, sources:sources + dirs] = jnp.sqrt(1.0 - u * u - v * v)

    pl.semaphore_wait(barrier, len(peers))

    pk_out = [
        copy(pk.at[me], pk.at[me], pk_send.at[i], pk_recv.at[me], peer)
        for i, peer in enumerate(peers)
    ]
    for c in pk_out:
        c.start()
    w_out = [
        copy(w_ref, wbuf.at[half], w_send.at[i], w_recv.at[half], h * 2 + core)
        for i, h in enumerate(halfs)
    ]
    for c in w_out:
        c.start()
    for i, peer in enumerate(peers):
        copy(pk.at[me], pk.at[peer], pk_send.at[i], pk_recv.at[peer], peer).wait_recv()

    for t in range(2):
        columns = jnp.transpose(pk[half * 2 + t])
        for j in range(3):
            pcol[j, t * points:(t + 1) * points, :] = jnp.broadcast_to(
                columns[0:points, j:j + 1], (points, LANES))
    columns = jnp.transpose(pk[me])
    fcol[...] = jnp.broadcast_to(columns[0:points, 3:4], (points, LANES))
    for t in range(GROUP):
        columns = jnp.transpose(pk[line * GROUP + t])
        for j in range(3):
            dcol[j, t * dirs:(t + 1) * dirs, :] = jnp.broadcast_to(
                columns[sources:sources + dirs, 4 + j:5 + j], (dirs, LANES))

    far_rows = GROUP * dirs

    def far(i, carry):
        at = lax.div(i, far_rows // ROWS)
        r = pl.multiple_of(lax.rem(i, far_rows // ROWS) * ROWS, ROWS)
        block = pk.at[at * GROUP + g]
        uc, vc, wc = dcol[0, pl.ds(r, ROWS), :], dcol[1, pl.ds(r, ROWS), :], dcol[2, pl.ds(r, ROWS), :]
        for j in range(points // LANES):
            lane = slice(j * LANES, (j + 1) * LANES)
            t = uc * block[0:1, lane] + vc * block[1:2, lane] + wc * block[2:3, lane]
            c, s = turn(t)
            fbuf[at, pl.ds(r, ROWS), lane] = c.astype(jnp.bfloat16)
            fbuf[at, pl.ds(far_rows + r, ROWS), lane] = s.astype(jnp.bfloat16)
        return carry

    near_rows = 2 * points

    def near(i, carry):
        at = lax.div(i, near_rows // ROWS)
        r = pl.multiple_of(lax.rem(i, near_rows // ROWS) * ROWS, ROWS)
        px, py, pz = pcol[0, pl.ds(r, ROWS), :], pcol[1, pl.ds(r, ROWS), :], pcol[2, pl.ds(r, ROWS), :]
        for y in range(2):
            block = pk.at[at * GROUP + y * 2 + core]
            for j in range(sources // LANES):
                lane = slice(j * LANES, (j + 1) * LANES)
                a = px - block[4:5, lane]
                b = py - block[5:6, lane]
                h = block[6:7, lane] - pz
                q = a * a + b * b + h * h
                inverse = lax.rsqrt(q)
                amplitude = (RANGE_REF * h) * (inverse * inverse)
                c, s = turn(q * inverse)
                to = slice(y * sources + j * LANES, y * sources + (j + 1) * LANES)
                gbuf[at, pl.ds(r, ROWS), to] = (amplitude * c).astype(jnp.bfloat16)
                gbuf[at, pl.ds(near_rows + r, ROWS), to] = (-amplitude * s).astype(jnp.bfloat16)
        return carry

    lax.fori_loop(0, lines * (near_rows // ROWS), near, 0)
    lax.fori_loop(0, lines * (far_rows // ROWS), far, 0)

    def weights_from(h):
        copy(w_ref, wbuf.at[h], w_send.at[0], w_recv.at[h], h * 2 + core).wait_recv()

    def near_dot(at):
        w = wbuf[pl.ds(at * 2, 2)].reshape(2 * sources, wbuf.shape[2])
        return jnp.dot(gbuf[at], w, preferred_element_type=jnp.float32)

    own_w.wait()
    weights_from(line * 2 + (1 - row))
    acc[...] = near_dot(line)

    def near_step(k, carry):
        at = lax.rem(line + k, lines)
        weights_from(at * 2)
        weights_from(at * 2 + 1)
        acc[...] += near_dot(at)
        return carry

    lax.fori_loop(1, lines, near_step, 0)

    def incident(t):
        r = pl.multiple_of(t * points, points)
        return acc[pl.ds(r, points), :] + rotate(acc[pl.ds(near_rows + r, points), :])

    give[...] = incident(1 - core)
    swap = copy(give, take, x_send, x_recv, partner)
    swap.start()
    mine[...] = incident(core)
    swap.wait_recv()
    cbuf[line] = ((mine[...] + take[...]) * fcol[...]).astype(jnp.bfloat16)

    c_out = [
        copy(cbuf.at[line], cbuf.at[line], c_send.at[k - 1], c_recv.at[line],
             lax.rem(line + k, lines) * GROUP + g)
        for k in range(1, lines)
    ]
    for c in c_out:
        c.start()

    acc2 = acc
    acc2[...] = jnp.dot(fbuf[line], cbuf[line], preferred_element_type=jnp.float32)

    def far_step(k, carry):
        at = lax.rem(line + k, lines)
        copy(cbuf.at[line], cbuf.at[at], c_send.at[0], c_recv.at[at], at * GROUP + g).wait_recv()
        acc2[...] += jnp.dot(fbuf[at], cbuf[at], preferred_element_type=jnp.float32)
        return carry

    lax.fori_loop(1, lines, far_step, 0)

    def pattern(t):
        r = pl.multiple_of(t * dirs, dirs)
        return acc2[pl.ds(r, dirs), :] + rotate(acc2[pl.ds(far_rows + r, dirs), :])

    others = [lax.rem(g + k, GROUP) for k in range(1, GROUP)]
    p_out = []
    for i, t in enumerate(others):
        psend[i] = pattern(t)
        c = copy(psend.at[i], precv.at[g], p_send.at[i], p_recv.at[g], line * GROUP + t)
        c.start()
        p_out.append(c)
    total = pattern(g)
    for i, t in enumerate(others):
        copy(psend.at[i], precv.at[t], p_send.at[i], p_recv.at[t], line * GROUP + t).wait_recv()
        total = total + precv[t]
    out_ref[...] = total

    for c in pk_out + w_out + [swap] + c_out + p_out:
        c.wait_send()


def per_device(
    feed_plane, feed_height, feed_weights, point_plane, point_height, patch_factor,
    direction_cosines,
):
    devices = lax.axis_size("refl")
    lines, halves = devices // GROUP, devices // 2
    points, sources, dirs = point_plane.shape[1], feed_plane.shape[1], direction_cosines.shape[1]
    columns = feed_weights.shape[1]
    width = max(points, sources + dirs)
    near_rows, far_rows = 2 * points, GROUP * dirs
    f32, bf16 = jnp.float32, jnp.bfloat16
    dma = pltpu.SemaphoreType.DMA
    vmem = pl.BlockSpec(memory_space=pltpu.VMEM)
    norm = 1.0 / math.sqrt(points * devices)
    return pl.pallas_call(
        functools.partial(kernel, devices, norm),
        out_shape=jax.ShapeDtypeStruct((dirs, columns), f32),
        in_specs=[vmem] * 6 + [pl.BlockSpec(memory_space=pl.ANY)],
        out_specs=vmem,
        scratch_shapes=[
            pltpu.VMEM((devices, 8, width), f32),
            pltpu.VMEM((halves, sources, columns), bf16),
            pltpu.VMEM((lines, 2 * near_rows, 2 * sources), bf16),
            pltpu.VMEM((lines, 2 * far_rows, points), bf16),
            pltpu.VMEM((3, near_rows, LANES), f32),
            pltpu.VMEM((3, far_rows, LANES), f32),
            pltpu.VMEM((points, LANES), f32),
            pltpu.VMEM((2 * max(near_rows, far_rows), columns), f32),
            pltpu.VMEM((points, columns), f32),
            pltpu.VMEM((points, columns), f32),
            pltpu.VMEM((points, columns), f32),
            pltpu.VMEM((lines, points, columns), bf16),
            pltpu.VMEM((GROUP - 1, dirs, columns), f32),
            pltpu.VMEM((GROUP, dirs, columns), f32),
            dma((halves + 1,)), dma((devices,)),
            dma((halves - 1,)), dma((halves,)), dma,
            dma, dma,
            dma((lines - 1,)), dma((lines,)),
            dma((GROUP - 1,)), dma((GROUP,)),
        ],
        compiler_params=pltpu.CompilerParams(collective_id=0, has_side_effects=True),
    )(
        point_plane, point_height.reshape(1, -1), patch_factor.reshape(1, -1),
        feed_plane, feed_height.reshape(1, -1), direction_cosines, feed_weights,
    )


def solution(mesh):
    in_specs = (
        P("grp", "refl"),
        P(("grp", "refl")),
        P("refl", "grp"),
        P("grp", "refl"),
        P(("grp", "refl")),
        P(("grp", "refl")),
        P(None, "refl"),
    )
    return jax.shard_map(
        per_device, mesh=mesh, in_specs=in_specs, out_specs=P("refl", "grp"), check_vma=False
    )
```

time: 150 us -> 35.5 us (0.24)
  blocking collectives: 97.8 us -> 0 us
  matrix products: 34.1 us -> 0 us
  Pallas kernels: 0 us -> 33.6 us
  between operations: 13.4 us -> 0.01 us
  other arithmetic: 2.98 us -> 0 us
    all_gather x5 -> x0, blocking collectives: 97.8 us -> none  [the longest x1 23.3 us: per_device(): lax.all_gather(feed_height, 'refl', axis=0, tiled=True)]
    dot_general x4 -> x0, matrix products: 34.1 us -> none  [the longest x1 9.56 us: incident_rows(): jnp.dot(quadrature, weights_turned, preferred_element_type=jnp.float32)]
    pallas_call x0 -> x1, Pallas kernels: none -> 33.6 us  [per_device(): pl.pallas_call(functools.partial(kernel, devices, norm), out_shape=jax.Sh...]
    neg x2 -> x0, other arithmetic: 2.29 us -> none  [rotate(): return jnp.concatenate([-columns[:, half:], columns[:, :half]], axis=1)]
  transfers between devices with their start and end apart: 1 -> 0, of which waited for: 0 -> 0; matrix products, arithmetic and copies ran while one was open for 0% -> 0% of each run, Pallas kernels for 0% -> 0%
where the time goes in v1:
time: 35.5 us; the launch traced here: 35.1 us
  Pallas kernels  33.6 us (95%)
  local copies, waits for them, and re-layouts  1.47 us (4%)
    pallas_call x1, Pallas kernels, per_device(): pl.pallas_call(functools.partial(kernel, devices, norm), out_shape=jax.Sh...  33.6 us
    unnamed x1, local copies, waits for them, and re-layouts  1.47 us

profile of v1, /device:TPU:0, one launch (start us, length us, event | category | flops | bytes accessed | tf_op | source)
XLA Modules:
  0.0 35.1 jit_solution(946909658520866303)
XLA Ops:
  0.0 33.6 %shard_map.73 = f32[128,128]{1,0:T(8,128)} custom-call(f32[2,256]{1,0:T(2,128)} %pp_ref.1, f32[1,256]{1,0:T(1,128)} %bitcast.3, f32[1,256]{1,0:T(1,128)} %bitcast.4, f32[2,128]{1,0:T(2,128)} %fp_ref.1, f32[1,128]{1,0:T(1,128)} %bitcast.5, f32[2,128]{1,0:T(2,128)} %dc_ref.1, bf16[128,128]{1,0:T(8,128)(2,1)} %w_ref.1), custom_call_target="tpu_custom_call" | custom-call | tf_op jit(solution)/shard_map/pallas_call | solution.py:236
  33.6 1.5 %copy.9 = f32[128,128]{1,0:T(8,128)} copy(f32[128,128]{1,0:T(8,128)} %shard_map.73) | data formatting | bytes 131072

commit v2 on v1

v2 whole, which is shorter than its diff:
```python
import functools
import math

import jax
import jax.numpy as jnp
from jax import lax
from jax.experimental import pallas as pl
from jax.experimental.pallas import tpu as pltpu
from jax.sharding import PartitionSpec as P

RANGE_REF = 20.0
GROUP = 4
LANES = 128
ROWS = 32
MESH = pl.DeviceIdType.MESH
ROUNDER = 12582912.0
COS = (1.4142135, -6.97885091, 5.73945958, -1.88355282, 0.310677863)
SIN = (4.44288292, -7.30824568, 3.60635403, -0.846110414, 0.109822044)


def horner(coefficients, x):
    total = coefficients[-1]
    for c in coefficients[-2::-1]:
        total = total * x + c
    return total


def turn(t):
    r = t - ((t + ROUNDER) - ROUNDER)
    x = r * r
    s = r * horner(SIN, x)
    return 1.0 - s * s, s * horner(COS, x)


def rotate(block):
    half = block.shape[1] // 2
    rolled = pltpu.roll(block, half, 1)
    lane = lax.broadcasted_iota(jnp.int32, block.shape, 1)
    return jnp.where(lane < half, -rolled, rolled)


def kernel(
    devices, norm,
    pp_in, ph_in, pf_in, fp_in, fh_in, dc_in, w_in, out_ref,
    pp_ref, ph_ref, pf_ref, fp_ref, fh_ref, dc_ref,
    pk, wbuf, gbuf, fbuf, pcol, dcol, fcol, acc, give, take, cbuf, psend, precv,
    in_sem, pk_send, pk_recv, w_send, w_recv, w_own, x_send, x_recv, p_send, p_recv,
):
    lines, halves = devices // GROUP, devices // 2
    points, sources, dirs = pp_in.shape[1], fp_in.shape[1], dc_in.shape[1]
    me = lax.axis_index("refl")
    line, g = lax.div(me, GROUP), lax.rem(me, GROUP)
    half, core = lax.div(me, 2), lax.rem(me, 2)
    row = lax.rem(half, 2)
    partner = half * 2 + (1 - core)
    beside = (line * 2 + (1 - row)) * 2 + core
    across = (line * 2 + (1 - row)) * 2 + (1 - core)

    def copy(src, dst, send, recv, to):
        return pltpu.make_async_remote_copy(
            src_ref=src, dst_ref=dst, send_sem=send, recv_sem=recv,
            device_id={"refl": to}, device_id_type=MESH,
        )

    offsets = sorted(range(1, lines), key=lambda k: (-min(k, lines - k), k))
    same_core = []
    for k in offsets:
        at = lax.rem(line + k, lines)
        same_core += [at * GROUP + (1 - row) * 2 + core, at * GROUP + g]
    same_core += [beside]
    peers = same_core + [across, partner]

    barrier = pltpu.get_barrier_semaphore()
    for peer in peers:
        pl.semaphore_signal(barrier, inc=1, device_id={"refl": peer}, device_id_type=MESH)
    own_w = pltpu.make_async_copy(w_in, wbuf.at[half], w_own)
    own_w.start()
    loads = [
        pltpu.make_async_copy(a, b, in_sem.at[i])
        for i, (a, b) in enumerate((
            (pp_in, pp_ref), (ph_in, ph_ref), (pf_in, pf_ref),
            (fp_in, fp_ref), (fh_in, fh_ref), (dc_in, dc_ref),
        ))
    ]
    for c in loads:
        c.start()
    for c in loads:
        c.wait()

    u, v = dc_ref[0:1, :], dc_ref[1:2, :]
    pk[me, :, :] = jnp.zeros((8, pk.shape[2]), jnp.float32)
    pk[me, 0:2, 0:points] = pp_ref[...]
    pk[me, 2:3, 0:points] = ph_ref[...]
    pk[me, 3:4, 0:points] = pf_ref[...] * norm
    pk[me, 4:6, 0:sources] = fp_ref[...]
    pk[me, 6:7, 0:sources] = fh_ref[...]
    pk[me, 4:6, sources:sources + dirs] = dc_ref[...]
    pk[me, 6:7, sources:sources + dirs] = jnp.sqrt(1.0 - u * u - v * v)

    pl.semaphore_wait(barrier, len(peers))

    pk_out = [
        copy(pk.at[me], pk.at[me], pk_send.at[i], pk_recv.at[me], peer)
        for i, peer in enumerate(peers)
    ]
    for c in pk_out:
        c.start()
    w_out = [
        copy(w_in, wbuf.at[half], w_send.at[i], w_recv.at[half], peer)
        for i, peer in enumerate(same_core)
    ]
    for c in w_out:
        c.start()

    def pack_from(peer):
        copy(pk.at[me], pk.at[peer], pk_send.at[0], pk_recv.at[peer], peer).wait_recv()

    for peer in (partner, beside, across):
        pack_from(peer)

    near_rows = GROUP * points
    for t in range(GROUP):
        columns = jnp.transpose(pk[line * GROUP + t])
        rows = slice(t * points, (t + 1) * points)
        for j in range(3):
            pcol[j, rows, :] = jnp.broadcast_to(columns[0:points, j:j + 1], (points, LANES))
        fcol[rows, :] = jnp.broadcast_to(columns[0:points, 3:4], (points, LANES))

    def near_block(at):
        def near(i, carry):
            r = pl.multiple_of(i * ROWS, ROWS)
            px, py, pz = pcol[0, pl.ds(r, ROWS), :], pcol[1, pl.ds(r, ROWS), :], pcol[2, pl.ds(r, ROWS), :]
            for y in range(2):
                block = pk.at[at * GROUP + y * 2 + core]
                for j in range(sources // LANES):
                    lane = slice(j * LANES, (j + 1) * LANES)
                    a = px - block[4:5, lane]
                    b = py - block[5:6, lane]
                    h = block[6:7, lane] - pz
                    q = a * a + b * b + h * h
                    inverse = lax.rsqrt(q)
                    amplitude = (RANGE_REF * h) * (inverse * inverse)
                    c, s = turn(q * inverse)
                    to = slice(y * sources + j * LANES, y * sources + (j + 1) * LANES)
                    gbuf[at, pl.ds(r, ROWS), to] = (amplitude * c).astype(jnp.bfloat16)
                    gbuf[at, pl.ds(near_rows + r, ROWS), to] = (-amplitude * s).astype(jnp.bfloat16)
            return carry

        lax.fori_loop(0, near_rows // ROWS, near, 0)

    def near_line(k, carry):
        at = lax.rem(line + k, lines)

        @pl.when(k > 0)
        def _():
            pack_from(at * GROUP + core)
            pack_from(at * GROUP + 2 + core)

        near_block(at)
        return carry

    lax.fori_loop(0, lines, near_line, 0)

    def weights_from(h):
        copy(w_in, wbuf.at[h], w_send.at[0], w_recv.at[h], h * 2 + core).wait_recv()

    def near_dot(at):
        w = wbuf[pl.ds(at * 2, 2)].reshape(2 * sources, wbuf.shape[2])
        return jnp.dot(gbuf[at], w, preferred_element_type=jnp.float32)

    own_w.wait()
    weights_from(line * 2 + (1 - row))
    acc[...] = near_dot(line)

    def near_step(k, carry):
        at = lax.rem(line + k, lines)
        weights_from(at * 2)
        weights_from(at * 2 + 1)
        acc[...] += near_dot(at)
        return carry

    lax.fori_loop(1, lines, near_step, 0)

    swaps = []
    for t in range(GROUP):
        rows = slice(t * points, (t + 1) * points)
        give[t] = acc[rows, :] + rotate(acc[near_rows + t * points:near_rows + (t + 1) * points, :])
        c = copy(give.at[t], take.at[t], x_send.at[t], x_recv.at[t], partner)
        c.start()
        swaps.append(c)

    def far_block(at):
        columns = jnp.transpose(pk[at * GROUP + g])
        for j in range(3):
            dcol[j] = jnp.broadcast_to(
                columns[sources:sources + dirs, 4 + j:5 + j], (dirs, LANES))

        def far(i, carry):
            t = lax.div(i, dirs // ROWS)
            r = pl.multiple_of(lax.rem(i, dirs // ROWS) * ROWS, ROWS)
            block = pk.at[line * GROUP + t]
            uc, vc, wc = dcol[0, pl.ds(r, ROWS), :], dcol[1, pl.ds(r, ROWS), :], dcol[2, pl.ds(r, ROWS), :]
            for j in range(points // LANES):
                lane = slice(j * LANES, (j + 1) * LANES)
                c, s = turn(uc * block[0:1, lane] + vc * block[1:2, lane] + wc * block[2:3, lane])
                fbuf[at, t, pl.ds(r, ROWS), lane] = c.astype(jnp.bfloat16)
                fbuf[at, t, pl.ds(dirs + r, ROWS), lane] = s.astype(jnp.bfloat16)
            return carry

        lax.fori_loop(0, GROUP * (dirs // ROWS), far, 0)

    def far_dot(at):
        both = jnp.dot(fbuf[at, 0], cbuf[0], preferred_element_type=jnp.float32)
        for t in range(1, GROUP):
            both += jnp.dot(fbuf[at, t], cbuf[t], preferred_element_type=jnp.float32)
        return both[0:dirs, :] + rotate(both[dirs:2 * dirs, :])

    order = [lax.rem(line + k, lines) for k in offsets]
    ahead = min(2, len(order))
    for at in order[:ahead]:
        far_block(at)

    for t in range(GROUP):
        swaps[t].wait_recv()
        rows = slice(t * points, (t + 1) * points)
        cbuf[t] = ((give[t] + take[t]) * fcol[rows, :]).astype(jnp.bfloat16)

    p_out = []
    for i, at in enumerate(order):
        if i >= ahead:
            far_block(at)
        psend[i] = far_dot(at).astype(jnp.bfloat16)
        c = copy(psend.at[i], precv.at[line], p_send.at[i], p_recv.at[line], at * GROUP + g)
        c.start()
        p_out.append(c)
    far_block(line)
    total = far_dot(line)
    for i, at in reversed(list(enumerate(order))):
        copy(psend.at[i], precv.at[at], p_send.at[i], p_recv.at[at], at * GROUP + g).wait_recv()
        total = total + precv[at].astype(jnp.float32)
    out_ref[...] = total

    for c in pk_out + w_out + swaps + p_out:
        c.wait_send()


def per_device(
    feed_plane, feed_height, feed_weights, point_plane, point_height, patch_factor,
    direction_cosines,
):
    devices = lax.axis_size("refl")
    lines, halves = devices // GROUP, devices // 2
    points, sources, dirs = point_plane.shape[1], feed_plane.shape[1], direction_cosines.shape[1]
    columns = feed_weights.shape[1]
    width = max(points, sources + dirs)
    near_rows = GROUP * points
    f32, bf16 = jnp.float32, jnp.bfloat16
    dma = pltpu.SemaphoreType.DMA
    norm = 1.0 / math.sqrt(points * devices)
    return pl.pallas_call(
        functools.partial(kernel, devices, norm),
        out_shape=jax.ShapeDtypeStruct((dirs, columns), f32),
        in_specs=[pl.BlockSpec(memory_space=pl.ANY)] * 7,
        out_specs=pl.BlockSpec(memory_space=pltpu.VMEM),
        scratch_shapes=[
            pltpu.VMEM((2, points), f32), pltpu.VMEM((1, points), f32), pltpu.VMEM((1, points), f32),
            pltpu.VMEM((2, sources), f32), pltpu.VMEM((1, sources), f32), pltpu.VMEM((2, dirs), f32),
            pltpu.VMEM((devices, 8, width), f32),
            pltpu.VMEM((halves, sources, columns), bf16),
            pltpu.VMEM((lines, 2 * near_rows, 2 * sources), bf16),
            pltpu.VMEM((lines, GROUP, 2 * dirs, points), bf16),
            pltpu.VMEM((3, near_rows, LANES), f32),
            pltpu.VMEM((3, dirs, LANES), f32),
            pltpu.VMEM((near_rows, LANES), f32),
            pltpu.VMEM((2 * near_rows, columns), f32),
            pltpu.VMEM((GROUP, points, columns), f32),
            pltpu.VMEM((GROUP, points, columns), f32),
            pltpu.VMEM((GROUP, points, columns), bf16),
            pltpu.VMEM((lines - 1, dirs, columns), bf16),
            pltpu.VMEM((lines, dirs, columns), bf16),
            dma((6,)), dma((halves + 1,)), dma((devices,)),
            dma((halves - 1,)), dma((halves,)), dma,
            dma((GROUP,)), dma((GROUP,)),
            dma((lines - 1,)), dma((lines,)),
        ],
        compiler_params=pltpu.CompilerParams(collective_id=0, has_side_effects=True),
    )(
        point_plane, point_height.reshape(1, -1), patch_factor.reshape(1, -1),
        feed_plane, feed_height.reshape(1, -1), direction_cosines, feed_weights,
    )


def solution(mesh):
    in_specs = (
        P("grp", "refl"),
        P(("grp", "refl")),
        P("refl", "grp"),
        P("grp", "refl"),
        P(("grp", "refl")),
        P(("grp", "refl")),
        P(None, "refl"),
    )
    return jax.shard_map(
        per_device, mesh=mesh, in_specs=in_specs, out_specs=P("refl", "grp"), check_vma=False
    )
```

time: 35.5 us -> 28.5 us (0.80)
  Pallas kernels: 33.6 us -> 26.8 us
    pallas_call x1, Pallas kernels: 33.6 us -> 26.8 us  [per_device(): pl.pallas_call(functools.partial(kernel, devices, norm), out_shape=jax.Sh...]
where the time goes in v2:
time: 28.5 us; the launch traced here: 28.2 us
  Pallas kernels  26.8 us (94%)
  local copies, waits for them, and re-layouts  1.47 us (5%)
    pallas_call x1, Pallas kernels, per_device(): pl.pallas_call(functools.partial(kernel, devices, norm), out_shape=jax.Sh...  26.8 us
    unnamed x1, local copies, waits for them, and re-layouts  1.47 us

profile of v2, /device:TPU:0, one launch (start us, length us, event | category | flops | bytes accessed | tf_op | source)
XLA Modules:
  0.0 28.2 jit_solution(13360180136414240140)
XLA Ops:
  0.0 26.8 %shard_map.73 = f32[128,128]{1,0:T(8,128)} custom-call(f32[2,256]{1,0:T(2,128)} %pp_in.1, f32[1,256]{1,0:T(1,128)} %bitcast.3, f32[1,256]{1,0:T(1,128)} %bitcast.4, f32[2,128]{1,0:T(2,128)} %fp_in.1, f32[1,128]{1,0:T(1,128)} %bitcast.5, f32[2,128]{1,0:T(2,128)} %dc_in.1, bf16[128,128]{1,0:T(8,128)(2,1)} %w_in.1), custom_call_target="tpu_custom_call" | custom-call | tf_op jit(solution)/shard_map/pallas_call | solution.py:260
  26.8 1.5 %copy.9 = f32[128,128]{1,0:T(8,128)} copy(f32[128,128]{1,0:T(8,128)} %shard_map.73) | data formatting | bytes 131072
